TPU v7x, 32 devices: a whole 2x2x4 slice. The times are simulated.
32 devices in a mesh: beam: 2 (over y), chan: 4 (over z), tgrp: 2 (over x), pol: 2 (over core).
Axes of the slice: x: 2, y: 2, z: 4, core: 2. Of those that a mesh axis runs over, the one named last changes fastest.
Arguments:
- voltages: bfloat16 [16, 8192, 512], P(('beam', 'chan', 'tgrp'), None, 'pol'), parts along dimension 0, may hold values from -6 to 6
- filter_taps: float32 [4, 8192], replicated, may hold values from -0.03125 to 0.03125
Outputs:
- visibility: float32 [512, 16, 2, 512], P('tgrp', ('beam', 'chan'), None, 'pol'), parts along dimension 1
There are 2 independent parts, one for each index of `beam`. A program takes and returns all parts, laid end to end along the dimension named above; an argument that names none is the same for every part. Nothing has to cross between parts.
All inputs are finite; a program needn't handle non-finite values.
Results may differ from a plain program's by a relative error of at most 0.013.
Values may be sent and summed in bfloat16 or wider, within the bound.
A program may use at most 64 MiB of HBM per device.

v0:
```python
import functools
import math

import jax
import jax.numpy as jnp
import numpy as np
from jax import lax
from jax.experimental import pallas as pl
from jax.experimental.pallas import tpu as pltpu
from jax.sharding import PartitionSpec as P

BAND_START = 1024
CH_DEV = 2
CHUNKS = 8
VMEM_BYTES = 64 * 2**20
SPARE_BYTES = 72 * 2**10
LINK = jnp.bfloat16
MESH = pl.DeviceIdType.MESH


def twiddle_table(length, chans):
    block, part, sub = np.meshgrid(np.arange(chans), np.arange(2), np.arange(CH_DEV), indexing="ij")
    channel = (BAND_START + block * CH_DEV + sub).reshape(-1, 1)
    angles = (channel * np.arange(length)[None] % length) * (2.0 * math.pi / length)
    is_real = part.reshape(-1, 1) == 0
    chunk = length // CHUNKS
    near, turn = angles[:, :chunk], angles[:, ::chunk]
    table = np.zeros((2 * len(angles), chunk + 128), np.float32)
    table[: len(angles), :chunk] = np.where(is_real, np.cos(near), -np.sin(near))
    table[len(angles) :, :chunk] = np.where(is_real, -np.sin(near), np.cos(near))
    table[: len(angles), chunk : chunk + CHUNKS] = np.cos(turn)
    table[len(angles) :, chunk : chunk + CHUNKS] = np.where(is_real, np.sin(turn), -np.sin(turn))
    return table


def tap_sum_matrix(frames, taps, swapped):
    rows, cols = CH_DEV * frames * 2, frames * taps * 2 * CH_DEV
    row = lax.broadcasted_iota(jnp.int32, (rows, cols), 0)
    col = lax.broadcasted_iota(jnp.int32, (rows, cols), 1)
    row_sub, row_frame, row_part = row // (2 * frames), row // 2 % frames, row % 2
    col_frame, col_tap = col // (taps * 2 * CH_DEV), col // (2 * CH_DEV) % taps
    col_part, col_sub = col // CH_DEV % 2, col % CH_DEV
    hit = (row_sub == col_sub) & (row_frame == col_frame + (taps - 1) - col_tap)
    if swapped:
        hit = hit & (row_part != col_part)
        value = jnp.where(row_part == 0, 1.0, -1.0)
    else:
        hit = hit & (row_part == col_part)
        value = jnp.float32(1.0)
    return jnp.where(hit, value, 0.0).astype(jnp.bfloat16)


def tap_summed(matrix, slots):
    flat = slots.reshape(slots.shape[0] * slots.shape[1], slots.shape[2])
    high = flat.astype(jnp.bfloat16)
    total = jnp.dot(matrix, high, preferred_element_type=jnp.float32)
    if flat.dtype == jnp.float32:
        low = (flat - high.astype(jnp.float32)).astype(jnp.bfloat16)
        total = total + jnp.dot(matrix, low, preferred_element_type=jnp.float32)
    return total.astype(jnp.bfloat16)


def power_kernel(frames, row_side, col_side, out_hbm, out_ref, wide_ref, sems):
    half = col_side.shape[1]
    rows = out_ref.shape[0] * 128 // (CH_DEV * 2 * half)
    tiles = half // 128
    stride = CH_DEV * 2 * tiles
    pieces = rows // 64 if rows == half else 1
    size = rows // pieces
    writes = []
    for piece in range(pieces):
        for part in range(2):
            for sub in range(CH_DEV):
                span = slice(sub * 2 * frames, (sub + 1) * 2 * frames)
                lanes = slice(piece * size, (piece + 1) * size) if rows == half else slice(None)
                vis = lax.dot_general(
                    row_side[part, span, lanes],
                    col_side[span],
                    (((0,), (0,)), ((), ())),
                    preferred_element_type=jnp.float32,
                ) * (1.0 / frames)
                if rows != half:
                    wide_ref[...] = vis
                    first = lax.axis_index("tgrp") * rows % half
                    vis = wide_ref[pl.ds(pl.multiple_of(first, 8), rows), :]
                for tile in range(tiles):
                    start = piece * size * stride + sub * 2 * tiles + tile * 2 + part
                    out_ref[pl.ds(start, size, stride=stride), :] = vis[:, tile * 128 : (tile + 1) * 128]
        region = pl.ds(piece * size * stride, size * stride)
        writes.append(pltpu.make_async_copy(out_ref.at[region], out_hbm.at[region], sems.at[piece]))
        writes[-1].start()
    for write in writes:
        write.wait()


def exchange_kernel(
    chans, groups, volt_hbm, taps_hbm, tw_hbm, rows_out, cols_out,
    volt, taps, tw, sent, cols, rows, load_sem, col_send, row_send, col_recv, row_recv,
):
    length, half = volt.shape
    tap_count = taps.shape[0]
    frames = chans * groups
    me_c, me_g, me_p = lax.axis_index("chan"), lax.axis_index("tgrp"), lax.axis_index("pol")
    me_f = me_c * groups + me_g
    per_half = groups // 2
    my_half = me_g // per_half
    chunk = length // CHUNKS
    per_block = 2 * CH_DEV

    loads = [
        pltpu.make_async_copy(taps_hbm, taps, load_sem.at[0]),
        pltpu.make_async_copy(tw_hbm, tw, load_sem.at[1]),
    ]
    for step in range(CHUNKS):
        span = pl.ds(step * chunk, chunk)
        loads.append(pltpu.make_async_copy(volt_hbm.at[0, span], volt.at[span], load_sem.at[2 + step]))
    for load in loads:
        load.start()

    barrier = pltpu.get_barrier_semaphore()
    for dc in range(chans):
        for dg in range(groups):
            for dp in range(2):
                if dc or dg or dp:
                    peer = {
                        "chan": lax.rem(me_c + dc, chans),
                        "tgrp": lax.rem(me_g + dg, groups),
                        "pol": lax.rem(me_p + dp, 2),
                    }
                    pl.semaphore_signal(barrier, inc=1, device_id=peer, device_id_type=MESH)

    matrix = tap_sum_matrix(frames, tap_count, False)
    both = jnp.concatenate([matrix, tap_sum_matrix(frames, tap_count, True)], 0)

    loads[0].wait()
    loads[1].wait()
    band_rows = tw.shape[0] // 2
    own, other = tw[:band_rows, :chunk], tw[band_rows:, :chunk]
    total = jnp.zeros((2 * tap_count * band_rows, half), jnp.float32)
    for step in range(CHUNKS):
        span = slice(step * chunk, (step + 1) * chunk)
        column = slice(chunk + step, chunk + step + 1)
        table = tw[:band_rows, column] * own + tw[band_rows:, column] * other
        gains = jnp.concatenate(
            [jnp.broadcast_to(taps[t : t + 1, span], (per_block, chunk)) for t in range(tap_count)], 0
        )
        wide = jnp.concatenate(
            [
                jnp.concatenate([table[b * per_block : (b + 1) * per_block]] * tap_count, 0) * gains
                for b in range(chans)
            ],
            0,
        )
        high = wide.astype(jnp.bfloat16)
        low = (wide - high.astype(jnp.float32)).astype(jnp.bfloat16)
        loads[2 + step].wait()
        total = total + jnp.dot(
            jnp.concatenate([high, low], 0), volt[span], preferred_element_type=jnp.float32
        )
    terms = total[: tap_count * band_rows] + total[tap_count * band_rows :]
    sent[...] = terms.reshape(sent.shape).astype(LINK)

    pl.semaphore_wait(barrier, chans * groups * 2 - 1)

    def col_copy(slot, to_c, to_g, index):
        return pltpu.make_async_remote_copy(
            src_ref=sent.at[to_c],
            dst_ref=cols.at[slot],
            send_sem=col_send.at[index],
            recv_sem=col_recv.at[slot],
            device_id={"chan": to_c, "tgrp": to_g, "pol": me_p},
            device_id_type=MESH,
        )

    def row_copy(slot, to_c, to_g, index):
        return pltpu.make_async_remote_copy(
            src_ref=sent.at[to_c],
            dst_ref=rows.at[slot],
            send_sem=row_send.at[index],
            recv_sem=row_recv.at[slot],
            device_id={"chan": to_c, "tgrp": to_g, "pol": 1 - me_p},
            device_id_type=MESH,
        )

    def each_send(act):
        for place in range(chans):
            to_c = jnp.where(me_c < chans // 2, chans - 1 - place, place)
            for dg in reversed(range(groups)):
                to_g = lax.rem(me_g + dg, groups)
                copy = col_copy(me_f, to_c, to_g, place * groups + dg)
                if dg:
                    act(copy)
                else:
                    pl.when(to_c != me_c)(functools.partial(act, copy))
            for member in range(per_half):
                act(row_copy(me_f, to_c, me_p * per_half + member, place * per_half + member))

    each_send(lambda copy: copy.start())
    cols[me_f] = sent[me_c]

    for dc in range(chans):
        for dg in range(groups):
            if dc or dg:
                from_c, from_g = lax.rem(me_c + dc, chans), lax.rem(me_g + dg, groups)
                col_copy(from_c * groups + from_g, me_c, me_g, 0).wait_recv()
    def put_rows(summed):
        rows_out[0] = summed[: matrix.shape[0]]
        rows_out[1] = summed[matrix.shape[0] :]

    @pl.when(my_half == me_p)
    def _():
        summed = tap_summed(both, cols[...])
        cols_out[...] = summed[: matrix.shape[0]]
        put_rows(summed)

    @pl.when(my_half != me_p)
    def _():
        cols_out[...] = tap_summed(matrix, cols[...])
        for source in range(frames):
            row_copy(source, me_c, me_g, 0).wait_recv()
        put_rows(tap_summed(both, rows[...]))

    each_send(lambda copy: copy.wait_send())


def body(voltages, filter_taps):
    chans, groups = lax.axis_size("chan"), lax.axis_size("tgrp")
    _, length, half = voltages.shape
    taps = filter_taps.shape[0]
    frames = chans * groups
    slot = taps * 2 * CH_DEV
    table = jnp.asarray(twiddle_table(length, chans))
    vmem = pl.BlockSpec(memory_space=pltpu.VMEM)
    summed = CH_DEV * 2 * frames
    row_side, col_side = pl.pallas_call(
        functools.partial(exchange_kernel, chans, groups),
        out_shape=(
            pltpu.VMEM((2, summed, half), jnp.bfloat16),
            pltpu.VMEM((summed, half), jnp.bfloat16),
        ),
        in_specs=[pl.BlockSpec(memory_space=pl.ANY)] * 3,
        out_specs=(vmem, vmem),
        scratch_shapes=[
            pltpu.VMEM((length, half), jnp.bfloat16),
            pltpu.VMEM(filter_taps.shape, jnp.float32),
            pltpu.VMEM(table.shape, jnp.float32),
            pltpu.VMEM((chans, slot, half), LINK),
            pltpu.VMEM((frames, slot, half), LINK),
            pltpu.VMEM((frames, slot, half), LINK),
            pltpu.SemaphoreType.DMA((2 + CHUNKS,)),
            pltpu.SemaphoreType.DMA((frames,)),
            pltpu.SemaphoreType.DMA((frames // 2,)),
            pltpu.SemaphoreType.DMA((frames,)),
            pltpu.SemaphoreType.DMA((frames,)),
        ],
        compiler_params=pltpu.CompilerParams(collective_id=0, has_side_effects=True, vmem_limit_bytes=VMEM_BYTES - SPARE_BYTES - 6 * summed * half),
        name="exchange",
    )(voltages, filter_taps, table)
    rows = half * lax.axis_size("pol") // groups
    tiles = half // 128
    powers = pl.pallas_call(
        functools.partial(power_kernel, frames),
        out_shape=jax.ShapeDtypeStruct((rows * CH_DEV * tiles * 2, 128), jnp.float32),
        in_specs=[vmem, vmem],
        out_specs=pl.BlockSpec(memory_space=pltpu.HBM),
        scratch_shapes=[
            pltpu.VMEM((rows * CH_DEV * tiles * 2, 128), jnp.float32),
            pltpu.VMEM((half, half) if rows != half else (8, 128), jnp.float32),
            pltpu.SemaphoreType.DMA((max(1, rows // 64),)),
        ],
        compiler_params=pltpu.CompilerParams(vmem_limit_bytes=VMEM_BYTES // 4),
        name="powers",
    )(row_side, col_side)
    powers = powers.reshape(rows, CH_DEV, tiles, 2, 128).transpose(0, 1, 3, 2, 4)
    return powers.reshape(rows, CH_DEV, 2, half)


def solution(mesh):
    return jax.shard_map(
        body,
        mesh=mesh,
        in_specs=(P(("beam", "chan", "tgrp"), None, "pol"), P()),
        out_specs=P("tgrp", ("beam", "chan"), None, "pol"),
        check_vma=False,
    )
```

profile of v0, /device:TPU:0, one launch (start us, length us, event | category | flops | bytes accessed | tf_op | source)
XLA Modules:
  0.0 12.3 jit_solution(7398003473923403343)
XLA Ops:
  0.0 11.1 %exchange.1 = (bf16[2,32,256]{2,1,0:T(8,128)(2,1)S(1)}, bf16[32,256]{1,0:T(8,128)(2,1)S(1)}) custom-call(bf16[1,8192,256]{2,1,0:T(8,128)(2,1)} %volt_hbm.1, f32[4,8192]{1,0:T(4,128)} %taps_hbm.1, f32[32,1152]{1,0:T(8,128)} %constant.2.clone.tw_hbm), custom_call_target="tpu_custom_call" | custom-call | tf_op jit(solution)/shard_map/exchange/pallas_call | solution.py:235
  11.1 1.2 %powers.1 = f32[2048,128]{1,0:T(8,128)} custom-call(bf16[2,32,256]{2,1,0:T(8,128)(2,1)S(1)} %get-tuple-element.7.row_side, bf16[32,256]{1,0:T(8,128)(2,1)S(1)} %get-tuple-element.8.col_side), custom_call_target="tpu_custom_call" | custom-call | tf_op jit(solution)/shard_map/powers/pallas_call | solution.py:261
where the time goes:
time: 12.5 us; the launch traced here: 12.3 us
  Pallas kernels  12.3 us (98%)
    pallas_call x1, Pallas kernels, body(): pl.pallas_call(functools.partial(exchange_kernel, chans, groups), out_sha...  11.1 us
    pallas_call x1, Pallas kernels, body(): pl.pallas_call(functools.partial(power_kernel, frames), out_shape=jax.Sha...  1.25 us

commit v1 on v0

v1 whole, which is shorter than its diff:
```python
import functools
import math

import jax
import jax.numpy as jnp
import numpy as np
from jax import lax
from jax.experimental import pallas as pl
from jax.experimental.pallas import tpu as pltpu
from jax.sharding import PartitionSpec as P

BAND_START = 1024
CH_DEV = 2
CHUNKS = 8
NEAR = 512
TILE = 256
VMEM_BYTES = 64 * 2**20
SPARE_BYTES = 72 * 2**10
LINK = jnp.bfloat16
MESH = pl.DeviceIdType.MESH


def twiddle_table(length, chans):
    axes = (np.arange(chans), np.arange(4 // CH_DEV), np.arange(2), np.arange(CH_DEV))
    block, _, part, sub = np.meshgrid(*axes, indexing="ij")
    channel = (BAND_START + block * CH_DEV + sub).reshape(-1, 1)
    angles = (channel * np.arange(length)[None] % length) * (2.0 * math.pi / length)
    is_real = part.reshape(-1, 1) == 0
    near, turn = angles[:, :NEAR], angles[:, ::NEAR]
    rows, turns = turn.shape
    table = np.zeros((2 * rows, NEAR + -(-turns // 128) * 128), np.float32)
    table[:rows, :NEAR] = np.where(is_real, np.cos(near), -np.sin(near))
    table[rows:, :NEAR] = np.where(is_real, -np.sin(near), np.cos(near))
    table[:rows, NEAR : NEAR + turns] = np.cos(turn)
    table[rows:, NEAR : NEAR + turns] = np.where(is_real, np.sin(turn), -np.sin(turn))
    return table


def tap_sum_matrix(frames, taps, swapped):
    rows, cols = CH_DEV * frames * 2, frames * taps * 2 * CH_DEV
    row = lax.broadcasted_iota(jnp.int32, (rows, cols), 0)
    col = lax.broadcasted_iota(jnp.int32, (rows, cols), 1)
    row_sub, row_frame, row_part = row // (2 * frames), row // 2 % frames, row % 2
    col_frame, col_tap = col // (taps * 2 * CH_DEV), col // (2 * CH_DEV) % taps
    col_part, col_sub = col // CH_DEV % 2, col % CH_DEV
    hit = (row_sub == col_sub) & (row_frame == col_frame + col_tap)
    if swapped:
        hit = hit & (row_part != col_part)
        value = jnp.where(row_part == 0, 1.0, -1.0)
    else:
        hit = hit & (row_part == col_part)
        value = jnp.float32(1.0)
    return jnp.where(hit, value, 0.0).astype(jnp.bfloat16)


def tap_summed(matrix, slots):
    flat = slots.reshape(slots.shape[0] * slots.shape[1], slots.shape[2])
    high = flat.astype(jnp.bfloat16)
    total = jnp.dot(matrix, high, preferred_element_type=jnp.float32)
    if flat.dtype == jnp.float32:
        low = (flat - high.astype(jnp.float32)).astype(jnp.bfloat16)
        total = total + jnp.dot(matrix, low, preferred_element_type=jnp.float32)
    return total.astype(jnp.bfloat16)


def power_kernel(row_terms, col_terms, out_hbm, out_ref, wide_ref, sems):
    frames, slot, half = col_terms.shape
    taps = slot // (2 * CH_DEV)
    matrix = tap_sum_matrix(frames, taps, False)
    both = jnp.concatenate([matrix, tap_sum_matrix(frames, taps, True)], 0)
    col_side = tap_summed(matrix, col_terms[...])
    row_side = tap_summed(both, row_terms[...])
    band = matrix.shape[0]
    rows = out_ref.shape[0] * 128 // (CH_DEV * 2 * half)
    tiles = half // 128
    stride = CH_DEV * 2 * tiles
    pieces = rows // 64 if rows == half else 1
    size = rows // pieces
    writes = []
    for piece in range(pieces):
        for part in range(2):
            for sub in range(CH_DEV):
                span = slice(sub * 2 * frames, (sub + 1) * 2 * frames)
                row_span = slice(part * band + span.start, part * band + span.stop)
                lanes = slice(piece * size, (piece + 1) * size) if rows == half else slice(None)
                vis = lax.dot_general(
                    row_side[row_span, lanes],
                    col_side[span],
                    (((0,), (0,)), ((), ())),
                    preferred_element_type=jnp.float32,
                ) * (1.0 / frames)
                if rows != half:
                    wide_ref[...] = vis
                    first = lax.axis_index("tgrp") * rows % half
                    vis = wide_ref[pl.ds(pl.multiple_of(first, 8), rows), :]
                for tile in range(tiles):
                    start = piece * size * stride + sub * 2 * tiles + tile * 2 + part
                    out_ref[pl.ds(start, size, stride=stride), :] = vis[:, tile * 128 : (tile + 1) * 128]
        region = pl.ds(piece * size * stride, size * stride)
        writes.append(pltpu.make_async_copy(out_ref.at[region], out_hbm.at[region], sems.at[piece]))
        writes[-1].start()
    for write in writes:
        write.wait()


def exchange_kernel(
    chans, groups, volt_hbm, taps_hbm, tw_hbm, row_terms, col_terms,
    volt, taps, tw, weights, sent, cols, rows, load_sem, col_send, row_send, col_recv, row_recv, ready,
):
    length, half = volt.shape
    tap_count = taps.shape[0]
    frames = chans * groups
    me_c, me_g, me_p = lax.axis_index("chan"), lax.axis_index("tgrp"), lax.axis_index("pol")
    me_f = me_c * groups + me_g
    me = me_f * 2 + me_p
    per_half = groups // 2
    my_half = me_g // per_half
    chunk = length // CHUNKS
    per_block = 2 * CH_DEV
    near = tap_count // 2
    late = frames - near

    def device(frame, pol):
        return {"chan": frame // groups, "tgrp": lax.rem(frame, groups), "pol": pol}

    loads = [
        pltpu.make_async_copy(taps_hbm, taps, load_sem.at[0]),
        pltpu.make_async_copy(tw_hbm, tw, load_sem.at[1]),
    ]
    for step in range(CHUNKS):
        span = pl.ds(step * chunk, chunk)
        loads.append(pltpu.make_async_copy(volt_hbm.at[0, span], volt.at[span], load_sem.at[2 + step]))
    for load in loads:
        load.start()

    barrier = pltpu.get_barrier_semaphore()

    @pl.loop(me + 1, frames * 2)
    def _(other):
        pl.semaphore_signal(barrier, inc=1, device_id=device(other // 2, lax.rem(other, 2)), device_id_type=MESH)

    pl.when(me > 0)(lambda: pl.semaphore_wait(barrier, me))
    takes_rows = my_half != me_p

    @pl.loop(0, me_f)
    def _(frame):
        pl.semaphore_signal(ready.at[me], inc=1, device_id=device(frame, me_p), device_id_type=MESH)

        @pl.when(takes_rows)
        def _():
            pl.semaphore_signal(ready.at[me], inc=1, device_id=device(frame, 1 - me_p), device_id_type=MESH)

    @pl.when(takes_rows & (me_p == 1))
    def _():
        pl.semaphore_signal(ready.at[me], inc=1, device_id=device(me_f, 1 - me_p), device_id_type=MESH)

    for slots in (cols, rows):
        slots[late:, near * per_block :, :] = jnp.zeros((near, (tap_count - near) * per_block, half), LINK)
    loads[0].wait()
    loads[1].wait()
    table_rows = tw.shape[0] // 2

    def compute(live):
        pairs = live * per_block // 8
        terms = pairs * table_rows
        own, other = tw[:table_rows, :NEAR], tw[table_rows:, :NEAR]
        first = lax.broadcasted_iota(jnp.int32, (8, NEAR), 0) < per_block
        for turn in range(length // NEAR):
            span = slice(turn * NEAR, (turn + 1) * NEAR)
            column = slice(NEAR + turn, NEAR + turn + 1)
            table = tw[:table_rows, column] * own + tw[table_rows:, column] * other
            gains = []
            for pair in range(pairs):
                t = tap_count - 1 - 2 * pair
                gains.append(
                    jnp.where(
                        first,
                        jnp.broadcast_to(taps[t : t + 1, span], (8, NEAR)),
                        jnp.broadcast_to(taps[t - 1 : t, span], (8, NEAR)),
                    )
                )
            wide = jnp.concatenate(
                [table[b * 8 : (b + 1) * 8] * gains[pair] for b in range(chans) for pair in range(pairs)], 0
            )
            high = wide.astype(jnp.bfloat16)
            weights[:terms, span] = high
            weights[terms : 2 * terms, span] = (wide - high.astype(jnp.float32)).astype(jnp.bfloat16)

        def multiply(*sums):
            for step in range(CHUNKS):
                loads[2 + step].wait()
                for tile in range(chunk // TILE):
                    place = step * (chunk // TILE) + tile
                    unit, stage = place % 2, place // 2 % 2
                    span = slice(place * TILE, (place + 1) * TILE)
                    pltpu.matmul_push_rhs(volt[span], stage, unit)
                    pltpu.matmul_acc_lhs(sums[unit], weights[: 2 * terms, span], load_staged_rhs=stage)
            return pltpu.matmul_pop(sums[0]) + pltpu.matmul_pop(sums[1])

        total = pl.run_scoped(
            multiply,
            pltpu.ACC(mxu_id=0)((2 * terms, half), jnp.float32),
            pltpu.ACC(mxu_id=1)((2 * terms, half), jnp.float32),
        )
        return (total[:terms] + total[terms:]).reshape(chans, live * per_block, half).astype(LINK)

    def col_copy(source, dest, live, index):
        span = pl.ds(0, live * per_block)
        return pltpu.make_async_remote_copy(
            src_ref=sent.at[dest // groups, span],
            dst_ref=cols.at[source, span],
            send_sem=col_send.at[index],
            recv_sem=col_recv.at[source],
            device_id=device(dest, me_p),
            device_id_type=MESH,
        )

    def row_copy(source, dest, live, index):
        span = pl.ds(0, live * per_block)
        return pltpu.make_async_remote_copy(
            src_ref=sent.at[dest // groups, span],
            dst_ref=rows.at[source, span],
            send_sem=row_send.at[index],
            recv_sem=row_recv.at[source],
            device_id=device(dest, 1 - me_p),
            device_id_type=MESH,
        )

    def feeds_rows(frame):
        return lax.rem(frame, groups) // per_half == me_p

    def start_all(live):
        def send_rows(frame, wait):
            @pl.when(feeds_rows(frame))
            def _():
                pl.when(wait)(lambda: pl.semaphore_wait(ready.at[frame * 2 + 1 - me_p], 1))
                row_copy(me_f, frame, live, frame).start()

        @pl.loop(0, me_f)
        def _(frame):
            col_copy(me_f, frame, live, frame).start()
            send_rows(frame, False)

        send_rows(me_f, me_p == 0)

        @pl.loop(me_f + 1, frames)
        def _(frame):
            pl.semaphore_wait(ready.at[frame * 2 + me_p], 1)
            col_copy(me_f, frame, live, frame).start()
            send_rows(frame, True)

    def wait_all(live):
        for frame in range(frames):
            pl.when(frame != me_f)(lambda: col_copy(me_f, frame, live, frame).wait_send())
            pl.when(feeds_rows(frame))(lambda: row_copy(me_f, frame, live, frame).wait_send())

    @pl.when(me_f < late)
    def _():
        sent[...] = compute(tap_count)
        start_all(tap_count)

    @pl.when(me_f >= late)
    def _():
        sent[:, : near * per_block, :] = compute(near)
        sent[:, near * per_block :, :] = jnp.zeros((chans, (tap_count - near) * per_block, half), LINK)
        start_all(near)

    cols[me_f] = sent[me_c]

    def live_of(source):
        return near if source >= late else tap_count

    def receive(sources):
        for source in sources:
            pl.when(source != me_f)(lambda: col_copy(source, me_f, live_of(source), 0).wait_recv())
            pl.when(takes_rows)(lambda: row_copy(source, me_f, live_of(source), 0).wait_recv())

    receive(range(late))
    pl.when(me_f < late)(lambda: wait_all(tap_count))
    pl.when(me_f >= late)(lambda: wait_all(near))
    receive(range(late, frames))

    col_terms[...] = cols[...]

    @pl.when(jnp.logical_not(takes_rows))
    def _():
        row_terms[...] = cols[...]

    @pl.when(takes_rows)
    def _():
        row_terms[...] = rows[...]


def body(voltages, filter_taps):
    chans, groups = lax.axis_size("chan"), lax.axis_size("tgrp")
    _, length, half = voltages.shape
    taps = filter_taps.shape[0]
    frames = chans * groups
    slot = taps * 2 * CH_DEV
    table = jnp.asarray(twiddle_table(length, chans))
    vmem = pl.BlockSpec(memory_space=pltpu.VMEM)
    row_terms, col_terms = pl.pallas_call(
        functools.partial(exchange_kernel, chans, groups),
        out_shape=(
            pltpu.VMEM((frames, slot, half), LINK),
            pltpu.VMEM((frames, slot, half), LINK),
        ),
        in_specs=[pl.BlockSpec(memory_space=pl.ANY)] * 3,
        out_specs=(vmem, vmem),
        scratch_shapes=[
            pltpu.VMEM((length, half), jnp.bfloat16),
            pltpu.VMEM(filter_taps.shape, jnp.float32),
            pltpu.VMEM(table.shape, jnp.float32),
            pltpu.VMEM((2 * chans * slot, length), jnp.bfloat16),
            pltpu.VMEM((chans, slot, half), LINK),
            pltpu.VMEM((frames, slot, half), LINK),
            pltpu.VMEM((frames, slot, half), LINK),
            pltpu.SemaphoreType.DMA((2 + CHUNKS,)),
            pltpu.SemaphoreType.DMA((frames,)),
            pltpu.SemaphoreType.DMA((frames,)),
            pltpu.SemaphoreType.DMA((frames,)),
            pltpu.SemaphoreType.DMA((frames,)),
            pltpu.SemaphoreType.REGULAR((frames * 2,)),
        ],
        compiler_params=pltpu.CompilerParams(collective_id=0, has_side_effects=True, vmem_limit_bytes=VMEM_BYTES - SPARE_BYTES - 4 * frames * slot * half),
        name="exchange",
    )(voltages, filter_taps, table)
    rows = half * lax.axis_size("pol") // groups
    tiles = half // 128
    powers = pl.pallas_call(
        power_kernel,
        out_shape=jax.ShapeDtypeStruct((rows * CH_DEV * tiles * 2, 128), jnp.float32),
        in_specs=[vmem, vmem],
        out_specs=pl.BlockSpec(memory_space=pltpu.HBM),
        scratch_shapes=[
            pltpu.VMEM((rows * CH_DEV * tiles * 2, 128), jnp.float32),
            pltpu.VMEM((half, half) if rows != half else (8, 128), jnp.float32),
            pltpu.SemaphoreType.DMA((max(1, rows // 64),)),
        ],
        compiler_params=pltpu.CompilerParams(vmem_limit_bytes=VMEM_BYTES // 4),
        name="powers",
    )(row_terms, col_terms)
    powers = powers.reshape(rows, CH_DEV, tiles, 2, 128).transpose(0, 1, 3, 2, 4)
    return powers.reshape(rows, CH_DEV, 2, half)


def solution(mesh):
    return jax.shard_map(
        body,
        mesh=mesh,
        in_specs=(P(("beam", "chan", "tgrp"), None, "pol"), P()),
        out_specs=P("tgrp", ("beam", "chan"), None, "pol"),
        check_vma=False,
    )
```

time: 12.5 us -> 12.2 us (0.976)
  Pallas kernels: 12.3 us -> 12 us
    pallas_call x1, Pallas kernels: 11.1 us -> 10.6 us  [body(): pl.pallas_call(functools.partial(exchange_kernel, chans, groups), out_sha...]
    pallas_call x1, Pallas kernels: 1.25 us -> 1.38 us  [body(): pl.pallas_call(power_kernel, out_shape=jax.ShapeDtypeStruct((rows * CH_DE...]
where the time goes in v1:
time: 12.2 us; the launch traced here: 12 us
  Pallas kernels  12 us (98%)
    pallas_call x1, Pallas kernels, body(): pl.pallas_call(functools.partial(exchange_kernel, chans, groups), out_sha...  10.6 us
    pallas_call x1, Pallas kernels, body(): pl.pallas_call(power_kernel, out_shape=jax.ShapeDtypeStruct((rows * CH_DE...  1.38 us

profile of v1, /device:TPU:0, one launch (start us, length us, event | category | flops | bytes accessed | tf_op | source)
XLA Modules:
  0.0 12.0 jit_solution(1278301207984270781)
XLA Ops:
  0.0 10.6 %exchange.1 = (bf16[8,16,256]{2,1,0:T(8,128)(2,1)S(1)}, bf16[8,16,256]{2,1,0:T(8,128)(2,1)S(1)}) custom-call(bf16[1,8192,256]{2,1,0:T(8,128)(2,1)} %volt_hbm.1, f32[4,8192]{1,0:T(4,128)} %taps_hbm.1, f32[64,640]{1,0:T(8,128)} %constant.2.clone.tw_hbm), custom_call_target="tpu_custom_call" | custom-call | tf_op jit(solution)/shard_map/exchange/pallas_call | solution.py:302
  10.6 1.4 %powers.1 = f32[2048,128]{1,0:T(8,128)} custom-call(bf16[8,16,256]{2,1,0:T(8,128)(2,1)S(1)} %get-tuple-element.7.row_terms, bf16[8,16,256]{2,1,0:T(8,128)(2,1)S(1)} %get-tuple-element.8.col_terms), custom_call_target="tpu_custom_call" | custom-call | tf_op jit(solution)/shard_map/powers/pallas_call | solution.py:330
